TPU v7x, 32 devices: a whole 2x2x4 slice. The times are simulated.
32 devices in a mesh: shard: 8 (over z, x), seq: 4 (over y, core).
Axes of the slice: x: 2, y: 2, z: 4, core: 2. Of those that a mesh axis runs over, the one named last changes fastest.
Arguments:
- inputs: bfloat16 [16, 512, 768], P('shard', 'seq'), may hold values from -6 to 6
- lengths: int32 [16], P('shard'), may hold values from 128 to 512, as said below
- w_query: bfloat16 [768, 768], P('shard'), may hold values from -0.21875 to 0.21875
- b_query: bfloat16 [768], P('shard'), may hold values from -3 to 3
- w_key: bfloat16 [768, 768], P('shard'), may hold values from -0.21875 to 0.21875
- w_value: bfloat16 [768, 768], P('shard'), may hold values from -0.21875 to 0.21875
- b_value: bfloat16 [768], P('shard'), may hold values from -2 to 2
- w_output: bfloat16 [768, 768], P('shard'), may hold values from -0.875 to 0.875
- b_output: bfloat16 [768], P('shard'), may hold values from -2 to 2
- gain_one: bfloat16 [768], P('shard'), may hold values from 0.25 to 1.75
- shift_one: bfloat16 [768], P('shard'), may hold values from -2 to 2
- w_inner: bfloat16 [768, 3072], P('shard'), may hold values from -0.21875 to 0.21875
- b_inner: bfloat16 [3072], P('shard'), may hold values from -2 to 2
- w_outer: bfloat16 [3072, 768], P('shard'), may hold values from -0.109375 to 0.109375
- b_outer: bfloat16 [768], P('shard'), may hold values from -2 to 2
- gain_two: bfloat16 [768], P('shard'), may hold values from 0.25 to 1.75
- shift_two: bfloat16 [768], P('shard'), may hold values from -2 to 2
- cotangent: bfloat16 [16, 512, 768], P('shard', 'seq'), may hold values from -6 to 6
Outputs:
- output: bfloat16 [16, 512, 768], P('shard', 'seq')
- grad_inputs: float32 [16, 512, 768], P('shard', 'seq')
- grad_w_query: float32 [768, 768], P('shard')
- grad_b_query: float32 [768], P('shard')
- grad_w_key: float32 [768, 768], P('shard')
- grad_w_value: float32 [768, 768], P('shard')
- grad_b_value: float32 [768], P('shard')
- grad_w_output: float32 [768, 768], P('shard')
- grad_b_output: float32 [768], P('shard')
- grad_gain_one: float32 [768], P('shard')
- grad_shift_one: float32 [768], P('shard')
- grad_w_inner: float32 [768, 3072], P('shard')
- grad_b_inner: float32 [3072], P('shard')
- grad_w_outer: float32 [3072, 768], P('shard')
- grad_b_outer: float32 [768], P('shard')
- grad_gain_two: float32 [768], P('shard')
- grad_shift_two: float32 [768], P('shard')
Inputs may be any that keep to these rules, and one draw needn't show every extreme that they name: `lengths`: every draw has a slot of 512 valid tokens and a slot of 128.
All inputs are finite; a program needn't handle non-finite values.
Results may differ from a plain program's by a relative error of at most 0.017.
Values may be sent and summed in bfloat16 or wider, within the bound.
A program may use at most 128 MiB of HBM per device.

v0:
```python
from functools import partial
import jax
import jax.numpy as jnp
from jax import lax
from jax.sharding import PartitionSpec as P

HEAD_DIM = 64
epsilon = 1e-12


def layer_norm(tensor, norm_gain, norm_shift):
    average = jnp.mean(tensor, axis=-1, keepdims=True)
    centred = tensor - average
    variance = jnp.mean(centred * centred, axis=-1, keepdims=True)
    return centred * lax.rsqrt(variance + epsilon) * norm_gain + norm_shift


def product(operand, weight):
    return jnp.dot(operand, weight, preferred_element_type=jnp.float32)


def row_contract(operand, weight):
    return lax.dot_general(
        operand, weight, (((0,), (0,)), ((), ())), preferred_element_type=jnp.float32
    )


def times_transposed(operand, weight):
    return lax.dot_general(
        operand, weight, (((1,), (1,)), ((), ())), preferred_element_type=jnp.float32
    )


def column_sum(tensor):
    return jnp.sum(tensor.astype(jnp.float32), axis=0)


def head_logits(query_seq, key_seq, length, factor):
    scores = (
        jnp.einsum("qhd,khd->hqk", query_seq, key_seq, preferred_element_type=jnp.float32) * factor
    )
    visible = jnp.arange(key_seq.shape[0]) < length
    return jnp.where(visible[None, None, :], scores, -1000000000.0)


def per_device(
    inputs,
    lengths,
    w_query,
    b_query,
    w_key,
    w_value,
    b_value,
    w_output,
    b_output,
    gain_one,
    shift_one,
    w_inner,
    b_inner,
    w_outer,
    b_outer,
    gain_two,
    shift_two,
    cotangent,
):
    local_seqs, tok_dev, model_width = inputs.shape
    groups = lax.axis_size("seq")
    head_width = model_width // groups
    local_heads = head_width // HEAD_DIM
    factor = HEAD_DIM ** (-0.5)
    gathered = (
        lax.all_gather(w_query, "shard", axis=0, tiled=True),
        lax.all_gather(b_query, "shard", axis=0, tiled=True),
        lax.all_gather(w_key, "shard", axis=0, tiled=True),
        lax.all_gather(w_value, "shard", axis=0, tiled=True),
        lax.all_gather(b_value, "shard", axis=0, tiled=True),
        lax.all_gather(w_output, "shard", axis=0, tiled=True),
        lax.all_gather(b_output, "shard", axis=0, tiled=True),
        lax.all_gather(gain_one, "shard", axis=0, tiled=True),
        lax.all_gather(shift_one, "shard", axis=0, tiled=True),
        lax.all_gather(w_inner, "shard", axis=0, tiled=True),
        lax.all_gather(b_inner, "shard", axis=0, tiled=True),
        lax.all_gather(w_outer, "shard", axis=0, tiled=True),
        lax.all_gather(b_outer, "shard", axis=0, tiled=True),
        lax.all_gather(gain_two, "shard", axis=0, tiled=True),
        lax.all_gather(shift_two, "shard", axis=0, tiled=True),
    )
    (
        query_w,
        query_b,
        key_w,
        value_w,
        value_b,
        output_w,
        output_b,
        gain_a,
        shift_a,
        inner_w,
        inner_b,
        outer_w,
        outer_b,
        gain_b,
        shift_b,
    ) = gathered
    gain_first = gain_a.astype(jnp.float32)
    shift_first = shift_a.astype(jnp.float32)
    gain_second = gain_b.astype(jnp.float32)
    shift_second = shift_b.astype(jnp.float32)
    flat_rows = inputs.reshape(local_seqs * tok_dev, model_width)
    queries = (product(flat_rows, query_w) + query_b.astype(jnp.float32)).astype(jnp.bfloat16)
    key_rows = product(flat_rows, key_w).astype(jnp.bfloat16)
    values = (product(flat_rows, value_w) + value_b.astype(jnp.float32)).astype(jnp.bfloat16)
    shape_seq = (local_seqs, tok_dev, model_width)
    head_q, head_k, head_v = (
        lax.all_to_all(queries.reshape(shape_seq), "seq", split_axis=2, concat_axis=1, tiled=True),
        lax.all_to_all(key_rows.reshape(shape_seq), "seq", split_axis=2, concat_axis=1, tiled=True),
        lax.all_to_all(values.reshape(shape_seq), "seq", split_axis=2, concat_axis=1, tiled=True),
    )
    seq_len = head_q.shape[1]
    split = (local_seqs, seq_len, local_heads, HEAD_DIM)
    head_q = head_q.reshape(split)
    head_k = head_k.reshape(split)
    head_v = head_v.reshape(split)

    def attend(packed):
        query_seq, key_seq, value_seq, length = packed
        logits = head_logits(query_seq, key_seq, length, factor)
        row_max = jnp.max(logits, axis=-1, keepdims=True)
        shifted = jnp.exp(logits - row_max)
        row_total = jnp.sum(shifted, axis=-1, keepdims=True)
        weights = (shifted / row_total).astype(jnp.bfloat16)
        context = jnp.einsum("hqk,khd->qhd", weights, value_seq, preferred_element_type=jnp.float32)
        return (context.astype(jnp.bfloat16), (row_max + jnp.log(row_total))[..., 0])

    head_context, log_total = lax.map(attend, (head_q, head_k, head_v, lengths))
    back_shape = (local_seqs, seq_len, head_width)
    context = lax.all_to_all(
        head_context.reshape(back_shape), "seq", split_axis=1, concat_axis=2, tiled=True
    ).reshape(-1, model_width)
    branch = product(context, output_w) + output_b.astype(jnp.float32)
    summed = flat_rows.astype(jnp.float32) + branch
    normed = layer_norm(summed, gain_first, shift_first)
    normed_low = normed.astype(jnp.bfloat16)
    pre_inner = product(normed_low, inner_w) + inner_b.astype(jnp.float32)
    activated = jax.nn.gelu(pre_inner, approximate=False).astype(jnp.bfloat16)
    final_sum = normed + product(activated, outer_w) + outer_b.astype(jnp.float32)
    result = layer_norm(final_sum, gain_second, shift_second)
    grad_out = cotangent.reshape(-1, model_width).astype(jnp.float32)
    second_back = jax.vjp(layer_norm, final_sum, gain_second, shift_second)[1]
    grad_final, grad_gain_two, grad_shift_two = second_back(grad_out)
    grad_ffn = grad_final.astype(jnp.bfloat16)
    grad_w_outer = row_contract(activated, grad_ffn)
    grad_b_outer = column_sum(grad_ffn)
    grad_active = times_transposed(grad_ffn, outer_w)
    gelu_back = jax.vjp(partial(jax.nn.gelu, approximate=False), pre_inner)[1]
    grad_pre = gelu_back(grad_active)[0].astype(jnp.bfloat16)
    grad_w_inner = row_contract(normed_low, grad_pre)
    grad_b_inner = column_sum(grad_pre)
    grad_normed = grad_final + times_transposed(grad_pre, inner_w)
    first_back = jax.vjp(layer_norm, summed, gain_first, shift_first)[1]
    grad_summed, grad_gain_one, grad_shift_one = first_back(grad_normed)
    grad_branch = grad_summed.astype(jnp.bfloat16)
    grad_w_output = row_contract(context, grad_branch)
    grad_b_output = column_sum(grad_branch)
    grad_context = times_transposed(grad_branch, output_w).astype(jnp.bfloat16)
    grad_head_context = lax.all_to_all(
        grad_context.reshape(shape_seq), "seq", split_axis=2, concat_axis=1, tiled=True
    ).reshape(split)

    def attend_back(packed):
        query_seq, key_seq, value_seq, log_sum, grad_seq, length = packed
        logits = head_logits(query_seq, key_seq, length, factor)
        attn_probs = jnp.exp(logits - log_sum[..., None])
        weights = attn_probs.astype(jnp.bfloat16)
        grad_value = jnp.einsum(
            "hqk,qhd->khd", weights, grad_seq, preferred_element_type=jnp.float32
        )
        grad_probs = jnp.einsum(
            "qhd,khd->hqk", grad_seq, value_seq, preferred_element_type=jnp.float32
        )
        inner_sum = jnp.sum(grad_probs * attn_probs, axis=-1, keepdims=True)
        grad_scores = (attn_probs * (grad_probs - inner_sum)).astype(jnp.bfloat16)
        grad_query = (
            jnp.einsum("hqk,khd->qhd", grad_scores, key_seq, preferred_element_type=jnp.float32)
            * factor
        )
        grad_key = (
            jnp.einsum("hqk,qhd->khd", grad_scores, query_seq, preferred_element_type=jnp.float32)
            * factor
        )
        return (
            grad_query.astype(jnp.bfloat16),
            grad_key.astype(jnp.bfloat16),
            grad_value.astype(jnp.bfloat16),
        )

    head_gq, head_gk, head_gv = lax.map(
        attend_back, (head_q, head_k, head_v, log_total, grad_head_context, lengths)
    )
    tok_gq, tok_gk, tok_gv = (
        lax.all_to_all(head_gq.reshape(back_shape), "seq", split_axis=1, concat_axis=2, tiled=True),
        lax.all_to_all(head_gk.reshape(back_shape), "seq", split_axis=1, concat_axis=2, tiled=True),
        lax.all_to_all(head_gv.reshape(back_shape), "seq", split_axis=1, concat_axis=2, tiled=True),
    )
    grad_query = tok_gq.reshape(-1, model_width)
    grad_key = tok_gk.reshape(-1, model_width)
    grad_value = tok_gv.reshape(-1, model_width)
    grad_w_query = row_contract(flat_rows, grad_query)
    grad_b_query = column_sum(grad_query)
    grad_w_key = row_contract(flat_rows, grad_key)
    grad_w_value = row_contract(flat_rows, grad_value)
    grad_b_value = column_sum(grad_value)
    grad_rows = (
        grad_summed
        + times_transposed(grad_query, query_w)
        + times_transposed(grad_key, key_w)
        + times_transposed(grad_value, value_w)
    )
    local_grads = (
        grad_w_query,
        grad_b_query,
        grad_w_key,
        grad_w_value,
        grad_b_value,
        grad_w_output,
        grad_b_output,
        grad_gain_one,
        grad_shift_one,
        grad_w_inner,
        grad_b_inner,
        grad_w_outer,
        grad_b_outer,
        grad_gain_two,
        grad_shift_two,
    )
    shares = (
        lax.psum_scatter(local_grads[0], "shard", scatter_dimension=0, tiled=True),
        lax.psum_scatter(local_grads[1], "shard", scatter_dimension=0, tiled=True),
        lax.psum_scatter(local_grads[2], "shard", scatter_dimension=0, tiled=True),
        lax.psum_scatter(local_grads[3], "shard", scatter_dimension=0, tiled=True),
        lax.psum_scatter(local_grads[4], "shard", scatter_dimension=0, tiled=True),
        lax.psum_scatter(local_grads[5], "shard", scatter_dimension=0, tiled=True),
        lax.psum_scatter(local_grads[6], "shard", scatter_dimension=0, tiled=True),
        lax.psum_scatter(local_grads[7], "shard", scatter_dimension=0, tiled=True),
        lax.psum_scatter(local_grads[8], "shard", scatter_dimension=0, tiled=True),
        lax.psum_scatter(local_grads[9], "shard", scatter_dimension=0, tiled=True),
        lax.psum_scatter(local_grads[10], "shard", scatter_dimension=0, tiled=True),
        lax.psum_scatter(local_grads[11], "shard", scatter_dimension=0, tiled=True),
        lax.psum_scatter(local_grads[12], "shard", scatter_dimension=0, tiled=True),
        lax.psum_scatter(local_grads[13], "shard", scatter_dimension=0, tiled=True),
        lax.psum_scatter(local_grads[14], "shard", scatter_dimension=0, tiled=True),
    )
    summed_grads = (
        lax.psum(shares[0].astype(jnp.bfloat16), "seq").astype(jnp.float32),
        lax.psum(shares[1].astype(jnp.bfloat16), "seq").astype(jnp.float32),
        lax.psum(shares[2].astype(jnp.bfloat16), "seq").astype(jnp.float32),
        lax.psum(shares[3].astype(jnp.bfloat16), "seq").astype(jnp.float32),
        lax.psum(shares[4].astype(jnp.bfloat16), "seq").astype(jnp.float32),
        lax.psum(shares[5].astype(jnp.bfloat16), "seq").astype(jnp.float32),
        lax.psum(shares[6].astype(jnp.bfloat16), "seq").astype(jnp.float32),
        lax.psum(shares[7].astype(jnp.bfloat16), "seq").astype(jnp.float32),
        lax.psum(shares[8].astype(jnp.bfloat16), "seq").astype(jnp.float32),
        lax.psum(shares[9].astype(jnp.bfloat16), "seq").astype(jnp.float32),
        lax.psum(shares[10].astype(jnp.bfloat16), "seq").astype(jnp.float32),
        lax.psum(shares[11].astype(jnp.bfloat16), "seq").astype(jnp.float32),
        lax.psum(shares[12].astype(jnp.bfloat16), "seq").astype(jnp.float32),
        lax.psum(shares[13].astype(jnp.bfloat16), "seq").astype(jnp.float32),
        lax.psum(shares[14].astype(jnp.bfloat16), "seq").astype(jnp.float32),
    )
    return (
        result.astype(jnp.bfloat16).reshape(shape_seq),
        grad_rows.reshape(shape_seq),
        summed_grads[0],
        summed_grads[1],
        summed_grads[2],
        summed_grads[3],
        summed_grads[4],
        summed_grads[5],
        summed_grads[6],
        summed_grads[7],
        summed_grads[8],
        summed_grads[9],
        summed_grads[10],
        summed_grads[11],
        summed_grads[12],
        summed_grads[13],
        summed_grads[14],
    )


def solution(mesh):
    return jax.shard_map(
        per_device,
        mesh=mesh,
        in_specs=(
            P("shard", "seq", None),
            P("shard"),
            P("shard", None),
            P("shard"),
            P("shard", None),
            P("shard", None),
            P("shard"),
            P("shard", None),
            P("shard"),
            P("shard"),
            P("shard"),
            P("shard", None),
            P("shard"),
            P("shard", None),
            P("shard"),
            P("shard"),
            P("shard"),
            P("shard", "seq", None),
        ),
        out_specs=(
            P("shard", "seq", None),
            P("shard", "seq", None),
            P("shard", None),
            P("shard"),
            P("shard", None),
            P("shard", None),
            P("shard"),
            P("shard", None),
            P("shard"),
            P("shard"),
            P("shard"),
            P("shard", None),
            P("shard"),
            P("shard", None),
            P("shard"),
            P("shard"),
            P("shard"),
        ),
        check_vma=False,
    )
```

profile of v0, /device:TPU:0, one launch (start us, length us, event | category | flops | bytes accessed | tf_op | source)
XLA Modules:
  0.0 1048.1 jit_solution(8084911402475072385)
XLA Ops:
  19.8 39.2 %all-reduce.18 = (bf16[768]{0:T(1024)(128)(2,1)S(1)}, bf16[768]{0:T(1024)(128)(2,1)S(1)}, bf16[768]{0:T(1024)(128)(2,1)S(1)}, bf16[768]{0:T(1024)(128)(2,1)S(1)}...) all-reduce(bf16[768]{0:T(1024)(128)(2,1)S(1)} %dynamic-update-slice, ...), channel_id=1, replica_groups=mesh['shard'=8,'seq'=4] {'shard'}, use_global_device_ids=true, to_apply=%add.1 | all-reduce | flops 6144 | bytes 24576
  65.6 30.7 %all-gather.10.cloned.1.call-done = bf16[768,768]{1,0:T(8,128)(2,1)} async-done(((bf16[96,768]{1,0:T(8,128)(2,1)}), bf16[768,768]{1,0:T(8,128)(2,1)}) %all-gather.10.cloned.1.call-update) | async-done | bytes 1179664 | tf_op jit(solution)/shard_map/all_gather | solution.py:72
  102.6 35.7 %all-gather.12.cloned.1.call-done = bf16[768,768]{1,0:T(8,128)(2,1)} async-done(((bf16[96,768]{1,0:T(8,128)(2,1)}), bf16[768,768]{1,0:T(8,128)(2,1)}) %all-gather.12.cloned.1.call-update) | async-done | bytes 1179664 | tf_op jit(solution)/shard_map/all_gather | solution.py:74
  145.7 6.3 all-to-all-done.2
  152.6 7.5 while.26
  164.7 26.5 %all-gather = bf16[8,1,384]{2,1,0:T(2,128)(2,1)S(1)} all-gather(bf16[1,1,384]{2,1,0:T(2,128)(2,1)S(1)} %reshape.251), channel_id=1, replica_groups=mesh['shard'=8,'seq'=4] {'shard'}, dimensions={0}, use_global_device_ids=true | all-gather | bytes 6912 | tf_op jit(solution)/shard_map/all_gather | solution.py:82
  194.9 65.5 %all-gather.16.cloned.1.call-done = bf16[768,3072]{1,0:T(8,128)(2,1)} async-done(((bf16[96,3072]{1,0:T(8,128)(2,1)}), bf16[768,3072]{1,0:T(8,128)(2,1)}) %all-gather.16.cloned.1.call-update) | async-done | bytes 4718608 | tf_op jit(solution)/shard_map/all_gather | solution.py:81
  260.4 12.1 %multiply_convert_fusion.1 = (bf16[256,3072]{1,0:T(8,128)(2,1)}, f32[256,3072]{1,0:T(8,128)}, f32[256,3072]{1,0:T(8,128)}) fusion(f32[3072]{0:T(1024)S(1)} %bitcast.275, bf16[768,3072]{1,0:T(8,128)(2,1)} %all-gather.16.cloned.1.call-done, f32[256,768]{1,0:T(8,128)S(1)} %get-tuple-element.290, f32[768]{0:T(1024)S(1)} %convert_element_type.217, ...), kind=kOutput, calls=%fused_computation.65 | convolution fusion | flops 1260847104 | bytes 13389824 | tf_op jit(solution)/shard_map/dot_general | solution.py:19
  272.4 67.7 %all-gather.18.cloned.1.call-done = bf16[3072,768]{1,0:T(8,128)(2,1)} async-done(((bf16[384,768]{1,0:T(8,128)(2,1)}), bf16[3072,768]{1,0:T(8,128)(2,1)}) %all-gather.18.cloned.1.call-update) | async-done | bytes 4718608 | tf_op jit(solution)/shard_map/all_gather | solution.py:83
  361.2 5.4 all-to-all-done.4
  367.9 14.8 %while.27 = (s32[]{:T(128)}, bf16[2,512,3,64]{1,3,2,0:T(8,128)(2,1)S(1)}, bf16[2,512,3,64]{1,3,2,0:T(8,128)(2,1)S(1)}, bf16[2,512,3,64]{1,3,2,0:T(8,128)(2,1)}, ...) while((s32[]{:T(128)}, ...), condition=%wide.region_14.15_spmd, body=%wide.region_12.14_spmd.sunk | while | flops 510884864 | bytes 28743872 | solution.py:197
  383.1 11.4 %all_to_all.120 = bf16[2,512,192]{2,0,1:T(2,128)(2,1)S(1)} all-to-all(bf16[2,512,192]{2,0,1:T(2,128)(2,1)S(1)} %copy.126), channel_id=1, replica_groups=mesh['shard'=8,'seq'=4] {'seq'}, dimensions={1} | all-to-all | bytes 786432 | tf_op jit(solution)/shard_map/all_to_all | solution.py:201
  400.9 11.2 %all_to_all.121 = bf16[2,512,192]{2,0,1:T(2,128)(2,1)S(1)} all-to-all(bf16[2,512,192]{2,0,1:T(2,128)(2,1)S(1)} %copy.129), channel_id=1, replica_groups=mesh['shard'=8,'seq'=4] {'seq'}, dimensions={1} | all-to-all | bytes 786432 | tf_op jit(solution)/shard_map/all_to_all | solution.py:202
  418.2 11.2 %all_to_all.122 = bf16[2,512,192]{2,0,1:T(2,128)(2,1)S(1)} all-to-all(bf16[2,512,192]{2,0,1:T(2,128)(2,1)S(1)} %copy.132), channel_id=1, replica_groups=mesh['shard'=8,'seq'=4] {'seq'}, dimensions={1} | all-to-all | bytes 786432 | tf_op jit(solution)/shard_map/all_to_all | solution.py:203
  435.7 6.4 fusion.88
  443.5 5.1 fusion.97
  451.2 35.5 %all-reduce.17 = (bf16[768]{0:T(1024)(128)(2,1)S(1)}, bf16[768]{0:T(1024)(128)(2,1)S(1)}, bf16[768]{0:T(1024)(128)(2,1)S(1)}, bf16[768]{0:T(1024)(128)(2,1)S(1)}...) all-reduce(f32[768]{0:T(1024)S(1)} %reduce_sum.190, ...), channel_id=3, replica_groups=mesh['shard'=8,'seq'=4] {'shard'}, use_global_device_ids=true, to_apply=%region_18.19.clone | all-reduce | flops 9216 | bytes 55296
  487.4 6.0 all-reduce.19
  499.7 5.1 reduce-scatter.19.cloned.1.call-done
  506.6 70.6 %reduce-scatter.21.cloned.1.call-done = f32[96,768]{1,0:T(8,128)} async-done(((f32[768,768]{1,0:T(8,128)}), f32[96,768]{1,0:T(8,128)}) %reduce-scatter.21.cloned.1.call-update) | async-done | bytes 294928
  579.0 70.6 %reduce-scatter.23.cloned.1.call-done = f32[96,768]{1,0:T(8,128)} async-done(((f32[768,768]{1,0:T(8,128)}), f32[96,768]{1,0:T(8,128)}) %reduce-scatter.23.cloned.1.call-update) | async-done | bytes 294928
  651.4 163.2 %reduce-scatter.15.cloned.1.call-done = f32[96,3072]{1,0:T(8,128)} async-done(((f32[768,3072]{1,0:T(8,128)}), f32[96,3072]{1,0:T(8,128)}) %reduce-scatter.15.cloned.1.call-update) | async-done | bytes 1179664 | tf_op jit(solution)/shard_map/reduce_scatter | solution.py:246
  816.8 162.5 %reduce-scatter.17.cloned.1.call-done = f32[384,768]{1,0:T(8,128)} async-done(((f32[3072,768]{1,0:T(8,128)}), f32[384,768]{1,0:T(8,128)}) %reduce-scatter.17.cloned.1.call-update) | async-done | bytes 1179664 | tf_op jit(solution)/shard_map/reduce_scatter | solution.py:248
  985.4 45.7 %all-reduce.23.cloned.1.call-done = (bf16[96,768]{0,1:T(8,128)(2,1)}, bf16[96,768]{0,1:T(8,128)(2,1)}, bf16[96,768]{0,1:T(8,128)(2,1)}, bf16[96,768]{1,0:T(8,128...) async-done(((bf16[96,768]{0,1:T(8,128)(2,1)}, bf16[96,768]{0,1:T(8,128)(2,1)}, bf16[96,768]{0,1:T(8,128)(2,1)}, bf16[96,768]{1,0:T(8,128)(2,1)}, ...) | async-done | bytes 1769488 | tf_op jit(solution)/shard_map/psum | solution.py:254
  (291 shorter events, 137.2 us)
Async XLA Ops:
  7.2 51.9 %all-gather.8.cloned.1.call-start = ((), (), s32[]{:S(2)}) async-start(), calls=%async_computation.14 | async-start | bytes 1327104 | tf_op jit(solution)/shard_map/all_gather | solution.py:75
  7.9 88.4 %all-gather.10.cloned.1.call-start = ((), (), s32[]{:S(2)}) async-start(), calls=%async_computation.15 | async-start | bytes 1327104 | tf_op jit(solution)/shard_map/all_gather | solution.py:72
  8.7 129.7 %all-gather.12.cloned.1.call-start = ((), (), s32[]{:S(2)}) async-start(), calls=%async_computation.16 | async-start | bytes 1327104 | tf_op jit(solution)/shard_map/all_gather | solution.py:74
  9.4 183.3 %all-gather.14.cloned.1.call-start = ((), (), s32[]{:S(2)}) async-start(), calls=%async_computation.17 | async-start | bytes 1327104 | tf_op jit(solution)/shard_map/all_gather | solution.py:77
  10.0 250.4 %all-gather.16.cloned.1.call-start = ((), (), s32[]{:S(2)}) async-start(), calls=%async_computation.18 | async-start | bytes 5308416 | tf_op jit(solution)/shard_map/all_gather | solution.py:81
  10.6 329.6 %all-gather.18.cloned.1.call-start = ((), (), s32[]{:S(2)}) async-start(), calls=%async_computation.19 | async-start | bytes 5308416 | tf_op jit(solution)/shard_map/all_gather | solution.py:83
  62.1 37.1 %all-to-all-start = ((bf16[2,128,768]{1,0,2:T(2,128)(2,1)}), bf16[2,128,768]{1,0,2:T(2,128)(2,1)S(1)}, u32[]{:S(2)}, u32[]{:S(2)}) async-start(bf16[2,128,768]{1,0,2:T(2,128)(2,1)} %copy.111), calls=%async_computation | async-start | bytes 786432 | tf_op jit(solution)/shard_map/all_to_all | solution.py:117
  99.2 42.0 %all-to-all-start.1 = ((bf16[2,128,768]{1,0,2:T(2,128)(2,1)}), bf16[2,128,768]{1,0,2:T(2,128)(2,1)S(1)}, u32[]{:S(2)}, u32[]{:S(2)}) async-start(bf16[2,128,768]{1,0,2:T(2,128)(2,1)} %copy.114), calls=%async_computation.1 | async-start | bytes 786432 | tf_op jit(solution)/shard_map/all_to_all | solution.py:115
  141.2 10.8 %all-to-all-start.2 = ((bf16[2,128,768]{1,0,2:T(2,128)(2,1)}), bf16[2,128,768]{1,0,2:T(2,128)(2,1)S(1)}, u32[]{:S(2)}, u32[]{:S(2)}) async-start(bf16[2,128,768]{1,0,2:T(2,128)(2,1)} %copy.117), calls=%async_computation.2 | async-start | bytes 786432 | tf_op jit(solution)/shard_map/all_to_all | solution.py:116
  161.2 30.1 %all-to-all-start.3 = ((bf16[2,512,192]{2,0,1:T(2,128)(2,1)}), bf16[2,512,192]{2,0,1:T(2,128)(2,1)S(1)}, u32[]{:S(2)}, u32[]{:S(2)}) async-start(bf16[2,512,192]{2,0,1:T(2,128)(2,1)} %copy.120), calls=%async_computation.3 | async-start | bytes 1048576 | tf_op jit(solution)/shard_map/all_to_all | solution.py:137
  194.6 157.6 %copy-start = (f32[256,768]{1,0:T(8,128)}, f32[256,768]{1,0:T(8,128)S(1)}, u32[]{:S(2)}) copy-start(f32[256,768]{1,0:T(8,128)S(1)} %get-tuple-element.290) | copy-start | bytes 2359300
  194.8 155.1 %copy-start.29 = (f32[256]{0:T(256)}, f32[256]{0:T(256)S(1)}, u32[]{:S(2)}) copy-start(f32[256]{0:T(256)S(1)} %fusion.86) | copy-start | bytes 3076
  355.7 10.8 %all-to-all-start.4 = ((bf16[2,128,768]{1,0,2:T(2,128)(2,1)}), bf16[2,128,768]{1,0,2:T(2,128)(2,1)S(1)}, u32[]{:S(2)}, u32[]{:S(2)}) async-start(bf16[2,128,768]{1,0,2:T(2,128)(2,1)} %copy.123), calls=%async_computation.4 | async-start | bytes 786432 | tf_op jit(solution)/shard_map/all_to_all | solution.py:166
  359.2 138.9 %reduce-scatter.13.cloned.1.call-start = ((), (), s32[]{:S(2)}) async-start(), calls=%async_computation.20 | async-start | bytes 2654208 | tf_op jit(solution)/shard_map/reduce_scatter | solution.py:242
  361.1 143.7 %reduce-scatter.19.cloned.1.call-start = ((), (), s32[]{:S(2)}) async-start(), calls=%async_computation.23 | async-start | bytes 2654208
  399.5 177.7 %reduce-scatter.21.cloned.1.call-start = ((), (), s32[]{:S(2)}) async-start(), calls=%async_computation.24 | async-start | bytes 2654208
  416.8 232.8 %reduce-scatter.23.cloned.1.call-start = ((), (), s32[]{:S(2)}) async-start(), calls=%async_computation.25 | async-start | bytes 2654208
  434.3 380.3 %reduce-scatter.15.cloned.1.call-start = ((), (), s32[]{:S(2)}) async-start(), calls=%async_computation.21 | async-start | bytes 10616832 | tf_op jit(solution)/shard_map/reduce_scatter | solution.py:246
  442.1 537.2 %reduce-scatter.17.cloned.1.call-start = ((), (), s32[]{:S(2)}) async-start(), calls=%async_computation.22 | async-start | bytes 10616832 | tf_op jit(solution)/shard_map/reduce_scatter | solution.py:248
  448.7 582.4 %all-reduce.23.cloned.1.call-start = ((), (), s32[]{:S(2)}) async-start(), calls=%async_computation.26 | async-start | bytes 3833856 | tf_op jit(solution)/shard_map/psum | solution.py:254
  506.6 474.8 %copy-start.14 = (bf16[2,128,4,192]{1,0,3,2:T(2,128)(2,1)S(1)}, bf16[2,128,4,192]{1,0,3,2:T(2,128)(2,1)}, u32[]{:S(2)}) copy-start(bf16[2,128,4,192]{1,0,3,2:T(2,128)(2,1)} %copy-done.13) | copy-start | bytes 1179652
  506.6 474.8 %copy-start.33 = (f32[256]{0:T(256)S(1)}, f32[256]{0:T(256)}, u32[]{:S(2)}) copy-start(f32[256]{0:T(256)} %copy-done.32) | copy-start | bytes 3076
  816.8 166.7 %copy-start.2 = (bf16[768,768]{1,0:T(8,128)(2,1)S(1)}, bf16[768,768]{1,0:T(8,128)(2,1)}, u32[]{:S(2)}) copy-start(bf16[768,768]{1,0:T(8,128)(2,1)} %all-gather.12.cloned.1.call-done) | copy-start | bytes 3538948
  816.8 166.7 %copy-start.4 = (bf16[2,128,4,192]{1,0,3,2:T(2,128)(2,1)S(1)}, bf16[2,128,4,192]{1,0,3,2:T(2,128)(2,1)}, u32[]{:S(2)}) copy-start(bf16[2,128,4,192]{1,0,3,2:T(2,128)(2,1)} %copy-done.3) | copy-start | bytes 1179652
  (40 other events, 241.8 us)
Sparse Core Ops, SparseCore 0:
  10.2 44.0 all-gather.7
  56.5 39.7 all-gather.9
  98.5 39.8 all-gather.11
  140.4 39.8 all-gather.13
  182.3 78.0 all-gather.15
  262.4 77.6 all-gather.17
  363.5 68.4 reduce-scatter.12
  435.5 69.3 reduce-scatter.18
  508.4 68.8 reduce-scatter.20
  580.6 68.9 reduce-scatter.22
  653.2 161.3 reduce-scatter.14
  818.0 161.1 reduce-scatter.16
  983.2 47.7 all-reduce.22
where the time goes:
time: 1060 us; the launch traced here: 1050 us
  waiting for transfers between devices  733 us (69%)
  blocking collectives  141 us (13%)
  matrix products  57.6 us (5%)
  local copies, waits for them, and re-layouts  55 us (5%)
  other arithmetic  26.5 us (2%)
  starting transfers between devices  17.8 us (2%)
  between operations  17 us (2%)
    reduce_scatter x1, waiting for transfers between devices, per_device(): lax.psum_scatter(local_grads[9], 'shard', scatter_dimension=0, tiled=True)  163 us
    reduce_scatter x1, waiting for transfers between devices, per_device(): lax.psum_scatter(local_grads[11], 'shard', scatter_dimension=0, tiled=True)  163 us
    unnamed x16, waiting for transfers between devices  150 us
    unnamed x2, blocking collectives  74.8 us
    all_gather x1, waiting for transfers between devices, per_device(): lax.all_gather(w_outer, 'shard', axis=0, tiled=True)  67.7 us
    all_gather x1, waiting for transfers between devices, per_device(): lax.all_gather(w_inner, 'shard', axis=0, tiled=True)  65.5 us
    psum x1, waiting for transfers between devices, per_device(): lax.psum(shares[0].astype(jnp.bfloat16), 'seq').astype(jnp.float32)  45.7 us
    all_gather x1, waiting for transfers between devices, per_device(): lax.all_gather(w_key, 'shard', axis=0, tiled=True)  35.7 us
  transfers between devices with their start and end apart: 18, of which 12 were waited for; matrix products, arithmetic and copies ran while one was open for 10% of the time, Pallas kernels for 0%

commit v1 on v0

--- a/solution.py
+++ b/solution.py
@@ -6,6 +6,27 @@
 
 HEAD_DIM = 64
 epsilon = 1e-12
+
+
+def gather_around(shard, axis, dim):
+    size, index, span = (lax.axis_size(axis), lax.axis_index(axis), shard.shape[dim])
+    forward = [(i, (i + 1) % size) for i in range(size)]
+    left = [(i, (i - 1) % size) for i in range(size)]
+    whole = jnp.zeros((*shard.shape[:dim], size * span, *shard.shape[dim + 1 :]), shard.dtype)
+    whole = lax.dynamic_update_slice_in_dim(whole, shard, index * span, axis=dim)
+    from_left = from_right = shard
+    half = size // 2
+    for hop in range(1, half + 1):
+        from_left = lax.ppermute(from_left, axis, forward)
+        whole = lax.dynamic_update_slice_in_dim(
+            whole, from_left, (index - hop) % size * span, axis=dim
+        )
+        if hop < size - half:
+            from_right = lax.ppermute(from_right, axis, left)
+            whole = lax.dynamic_update_slice_in_dim(
+                whole, from_right, (index + hop) % size * span, axis=dim
+            )
+    return whole
 
 
 def layer_norm(tensor, norm_gain, norm_shift):
@@ -69,7 +90,7 @@
     local_heads = head_width // HEAD_DIM
     factor = HEAD_DIM ** (-0.5)
     gathered = (
-        lax.all_gather(w_query, "shard", axis=0, tiled=True),
+        gather_around(w_query, "shard", 0),
         lax.all_gather(b_query, "shard", axis=0, tiled=True),
         lax.all_gather(w_key, "shard", axis=0, tiled=True),
         lax.all_gather(w_value, "shard", axis=0, tiled=True),

time: 1060 us -> 1020 us (0.962)
  waiting for transfers between devices: 733 us -> 671 us
  starting transfers between devices: 17.8 us -> 34.5 us
    all_gather x1, waiting for transfers between devices: 35.7 us -> 0.02 us  [per_device(): lax.all_gather(w_key, 'shard', axis=0, tiled=True)]
    all_gather x1 -> x0, waiting for transfers between devices: 30.7 us -> none  [per_device(): lax.all_gather(w_query, 'shard', axis=0, tiled=True)]
    all_gather x1, waiting for transfers between devices: 65.5 us -> 47.4 us  [per_device(): lax.all_gather(w_inner, 'shard', axis=0, tiled=True)]
    ppermute x0 -> x7, starting transfers between devices: none -> 16.7 us  [the longest x3 11.3 us: gather_around(): from_right = lax.ppermute(from_right, axis, left)]
    ppermute x0 -> x7, waiting for transfers between devices: none -> 14.3 us  [the longest x4 14.2 us: gather_around(): from_left = lax.ppermute(from_left, axis, forward)]
    all_gather x1, blocking collectives: 26.5 us -> 38.6 us  [per_device(): lax.all_gather(b_inner, 'shard', axis=0, tiled=True)]
    unnamed x120 -> x130, local copies, waits for them, and re-layouts: 31.2 us -> 29.4 us
    unnamed x16 -> x15, waiting for transfers between devices: 150 us -> 149 us
  transfers between devices with their start and end apart: 18 -> 24, of which waited for: 12 -> 16; matrix products, arithmetic and copies ran while one was open for 10% -> 10% of each run, Pallas kernels for 0% -> 0%
where the time goes in v1:
time: 1020 us; the launch traced here: 1010 us
  waiting for transfers between devices  671 us (66%)
  blocking collectives  149 us (15%)
  matrix products  56.9 us (6%)
  local copies, waits for them, and re-layouts  52 us (5%)
  starting transfers between devices  34.5 us (3%)
  other arithmetic  26.7 us (3%)
  between operations  17.8 us (2%)
    reduce_scatter x1, waiting for transfers between devices, per_device(): lax.psum_scatter(local_grads[9], 'shard', scatter_dimension=0, tiled=True)  163 us
    reduce_scatter x1, waiting for transfers between devices, per_device(): lax.psum_scatter(local_grads[11], 'shard', scatter_dimension=0, tiled=True)  163 us
    unnamed x15, waiting for transfers between devices  149 us
    unnamed x2, blocking collectives  70.4 us
    all_gather x1, waiting for transfers between devices, per_device(): lax.all_gather(w_outer, 'shard', axis=0, tiled=True)  68.1 us
    all_gather x1, waiting for transfers between devices, per_device(): lax.all_gather(w_inner, 'shard', axis=0, tiled=True)  47.4 us
    psum x1, waiting for transfers between devices, per_device(): lax.psum(shares[0].astype(jnp.bfloat16), 'seq').astype(jnp.float32)  45.8 us
    all_gather x1, blocking collectives, per_device(): lax.all_gather(b_inner, 'shard', axis=0, tiled=True)  38.6 us
  transfers between devices with their start and end apart: 24, of which 16 were waited for; matrix products, arithmetic and copies ran while one was open for 10% of the time, Pallas kernels for 0%

profile of v1, /device:TPU:0, one launch (start us, length us, event | category | flops | bytes accessed | tf_op | source)
XLA Modules:
  0.0 1007.8 jit_solution(11591582794456072031)
XLA Ops:
  25.0 35.0 %all-reduce.18 = (bf16[768]{0:T(1024)(128)(2,1)S(1)}, bf16[768]{0:T(1024)(128)(2,1)S(1)}, bf16[768]{0:T(1024)(128)(2,1)S(1)}, bf16[768]{0:T(1024)(128)(2,1)S(1)}...) all-reduce(bf16[768]{0:T(1024)(128)(2,1)S(1)} %dynamic-update-slice, ...), channel_id=1, replica_groups=mesh['shard'=8,'seq'=4] {'shard'}, use_global_device_ids=true, to_apply=%add.1 | all-reduce | flops 6144 | bytes 24576
  60.2 4.7 collective-permute-start.3
  77.7 7.4 collective-permute-done.6
  114.0 6.3 all-to-all-done.2
  120.9 7.5 while.26
  133.0 38.6 %all-gather = bf16[8,1,384]{2,1,0:T(2,128)(2,1)S(1)} all-gather(bf16[1,1,384]{2,1,0:T(2,128)(2,1)S(1)} %reshape.251), channel_id=1, replica_groups=mesh['shard'=8,'seq'=4] {'shard'}, dimensions={0}, use_global_device_ids=true | all-gather | bytes 6912 | tf_op jit(solution)/shard_map/all_gather | solution.py:103
  175.3 47.4 %all-gather.13.cloned.1.call-done = bf16[768,3072]{1,0:T(8,128)(2,1)} async-done(((bf16[96,3072]{1,0:T(8,128)(2,1)}), bf16[768,3072]{1,0:T(8,128)(2,1)}) %all-gather.13.cloned.1.call-update) | async-done | bytes 4718608 | tf_op jit(solution)/shard_map/all_gather | solution.py:102
  222.7 11.7 %multiply_convert_fusion.1 = (bf16[256,3072]{1,0:T(8,128)(2,1)}, f32[256,3072]{1,0:T(8,128)}, f32[256,3072]{1,0:T(8,128)}) fusion(f32[3072]{0:T(1024)S(1)} %bitcast.276, bf16[768,3072]{1,0:T(8,128)(2,1)} %all-gather.13.cloned.1.call-done, f32[256,768]{1,0:T(8,128)S(1)} %get-tuple-element.290, f32[768]{0:T(1024)S(1)} %convert_element_type.221, ...), kind=kOutput, calls=%fused_computation.65 | convolution fusion | flops 1260847104 | bytes 13389824 | tf_op jit(solution)/shard_map/dot_general | solution.py:40
  234.3 68.1 %all-gather.15.cloned.1.call-done = bf16[3072,768]{1,0:T(8,128)(2,1)} async-done(((bf16[384,768]{1,0:T(8,128)(2,1)}), bf16[3072,768]{1,0:T(8,128)(2,1)}) %all-gather.15.cloned.1.call-update) | async-done | bytes 4718608 | tf_op jit(solution)/shard_map/all_gather | solution.py:104
  323.4 5.4 all-to-all-done.4
  330.2 14.6 %while.27 = (s32[]{:T(128)}, bf16[2,512,3,64]{1,3,2,0:T(8,128)(2,1)S(1)}, bf16[2,512,3,64]{1,3,2,0:T(8,128)(2,1)S(1)}, bf16[2,512,3,64]{1,3,2,0:T(8,128)(2,1)}, ...) while((s32[]{:T(128)}, ...), condition=%wide.region_14.15_spmd, body=%wide.region_12.14_spmd.sunk | while | flops 510884864 | bytes 25598080 | solution.py:218
  345.2 11.2 %all_to_all.120 = bf16[2,512,192]{2,0,1:T(2,128)(2,1)S(1)} all-to-all(bf16[2,512,192]{2,0,1:T(2,128)(2,1)S(1)} %copy.126), channel_id=1, replica_groups=mesh['shard'=8,'seq'=4] {'seq'}, dimensions={1} | all-to-all | bytes 786432 | tf_op jit(solution)/shard_map/all_to_all | solution.py:222
  362.8 11.2 %all_to_all.121 = bf16[2,512,192]{2,0,1:T(2,128)(2,1)S(1)} all-to-all(bf16[2,512,192]{2,0,1:T(2,128)(2,1)S(1)} %copy.129), channel_id=1, replica_groups=mesh['shard'=8,'seq'=4] {'seq'}, dimensions={1} | all-to-all | bytes 786432 | tf_op jit(solution)/shard_map/all_to_all | solution.py:223
  380.1 11.2 %all_to_all.122 = bf16[2,512,192]{2,0,1:T(2,128)(2,1)S(1)} all-to-all(bf16[2,512,192]{2,0,1:T(2,128)(2,1)S(1)} %copy.132), channel_id=1, replica_groups=mesh['shard'=8,'seq'=4] {'seq'}, dimensions={1} | all-to-all | bytes 786432 | tf_op jit(solution)/shard_map/all_to_all | solution.py:224
  397.7 6.3 fusion.90
  405.5 5.1 fusion.99
  413.1 35.4 %all-reduce.17 = (bf16[768]{0:T(1024)(128)(2,1)S(1)}, bf16[768]{0:T(1024)(128)(2,1)S(1)}, bf16[768]{0:T(1024)(128)(2,1)S(1)}, bf16[768]{0:T(1024)(128)(2,1)S(1)}...) all-reduce(f32[768]{0:T(1024)S(1)} %reduce_sum.190, ...), channel_id=3, replica_groups=mesh['shard'=8,'seq'=4] {'shard'}, use_global_device_ids=true, to_apply=%region_18.19.clone | all-reduce | flops 9216 | bytes 55296
  449.1 6.4 all-reduce.19
  461.8 4.9 reduce-scatter.19.cloned.1.call-done
  468.5 70.6 %reduce-scatter.21.cloned.1.call-done = f32[96,768]{1,0:T(8,128)} async-done(((f32[768,768]{1,0:T(8,128)}), f32[96,768]{1,0:T(8,128)}) %reduce-scatter.21.cloned.1.call-update) | async-done | bytes 294928
  540.9 70.6 %reduce-scatter.23.cloned.1.call-done = f32[96,768]{1,0:T(8,128)} async-done(((f32[768,768]{1,0:T(8,128)}), f32[96,768]{1,0:T(8,128)}) %reduce-scatter.23.cloned.1.call-update) | async-done | bytes 294928
  613.3 163.0 %reduce-scatter.15.cloned.1.call-done = f32[96,3072]{1,0:T(8,128)} async-done(((f32[768,3072]{1,0:T(8,128)}), f32[96,3072]{1,0:T(8,128)}) %reduce-scatter.15.cloned.1.call-update) | async-done | bytes 1179664 | tf_op jit(solution)/shard_map/reduce_scatter | solution.py:267
  778.5 162.7 %reduce-scatter.17.cloned.1.call-done = f32[384,768]{1,0:T(8,128)} async-done(((f32[3072,768]{1,0:T(8,128)}), f32[384,768]{1,0:T(8,128)}) %reduce-scatter.17.cloned.1.call-update) | async-done | bytes 1179664 | tf_op jit(solution)/shard_map/reduce_scatter | solution.py:269
  947.0 45.8 %all-reduce.23.cloned.1.call-done = (bf16[96,768]{0,1:T(8,128)(2,1)}, bf16[96,768]{0,1:T(8,128)(2,1)}, bf16[96,768]{0,1:T(8,128)(2,1)}, bf16[96,768]{1,0:T(8,128...) async-done(((bf16[96,768]{0,1:T(8,128)(2,1)}, bf16[96,768]{0,1:T(8,128)(2,1)}, bf16[96,768]{0,1:T(8,128)(2,1)}, bf16[96,768]{1,0:T(8,128)(2,1)}, ...) | async-done | bytes 1769488 | tf_op jit(solution)/shard_map/psum | solution.py:275
  (313 shorter events, 161.0 us)
Async XLA Ops:
  7.2 84.1 %all-gather.7.cloned.1.call-start = ((), (), s32[]{:S(2)}) async-start(), calls=%async_computation.14 | async-start | bytes 1327104 | tf_op jit(solution)/shard_map/all_gather | solution.py:96
  7.9 94.2 %all-gather.9.cloned.1.call-start = ((), (), s32[]{:S(2)}) async-start(), calls=%async_computation.15 | async-start | bytes 1327104 | tf_op jit(solution)/shard_map/all_gather | solution.py:95
  8.7 164.5 %all-gather.11.cloned.1.call-start = ((), (), s32[]{:S(2)}) async-start(), calls=%async_computation.16 | async-start | bytes 1327104 | tf_op jit(solution)/shard_map/all_gather | solution.py:98
  9.4 213.2 %all-gather.13.cloned.1.call-start = ((), (), s32[]{:S(2)}) async-start(), calls=%async_computation.17 | async-start | bytes 5308416 | tf_op jit(solution)/shard_map/all_gather | solution.py:102
  10.0 292.4 %all-gather.15.cloned.1.call-start = ((), (), s32[]{:S(2)}) async-start(), calls=%async_computation.18 | async-start | bytes 5308416 | tf_op jit(solution)/shard_map/all_gather | solution.py:104
  10.0 50.1 %collective-permute-start = (bf16[96,768]{1,0:T(8,128)(2,1)}, bf16[96,768]{1,0:T(8,128)(2,1)S(1)}, u32[]{:S(2)}, u32[]{:S(2)}) collective-permute-start(bf16[96,768]{1,0:T(8,128)(2,1)} %param.24), channel_id=1, source_target_pairs={{0,4},{4,8},{8,12},{12,16},{16,20},{20,24},{24,28},{28,0},{1,5},{5... | collective-permute-start | bytes 442376 | tf_op jit(solution)/shard_map/ppermute | solution.py:20
  13.1 47.2 %collective-permute-start.1 = (bf16[96,768]{1,0:T(8,128)(2,1)}, bf16[96,768]{1,0:T(8,128)(2,1)S(1)}, u32[]{:S(2)}, u32[]{:S(2)}) collective-permute-start(bf16[96,768]{1,0:T(8,128)(2,1)} %param.24), channel_id=1, source_target_pairs={{0,28},{4,0},{8,4},{12,8},{16,12},{20,16},{24,20},{28,24},{1,29},{... | collective-permute-start | bytes 442376 | tf_op jit(solution)/shard_map/ppermute | solution.py:25
  60.2 8.0 collective-permute-start.2
  60.2 9.9 collective-permute-start.3
  68.2 9.1 collective-permute-start.4
  70.2 7.6 collective-permute-start.5
  77.3 7.8 collective-permute-start.6
  87.8 10.8 %all-to-all-start.1 = ((bf16[2,128,768]{1,0,2:T(2,128)(2,1)}), bf16[2,128,768]{1,0,2:T(2,128)(2,1)S(1)}, u32[]{:S(2)}, u32[]{:S(2)}) async-start(bf16[2,128,768]{1,0,2:T(2,128)(2,1)} %copy.114), calls=%async_computation.1 | async-start | bytes 786432 | tf_op jit(solution)/shard_map/all_to_all | solution.py:136
  98.6 10.8 %all-to-all-start = ((bf16[2,128,768]{1,0,2:T(2,128)(2,1)}), bf16[2,128,768]{1,0,2:T(2,128)(2,1)S(1)}, u32[]{:S(2)}, u32[]{:S(2)}) async-start(bf16[2,128,768]{1,0,2:T(2,128)(2,1)} %copy.111), calls=%async_computation | async-start | bytes 786432 | tf_op jit(solution)/shard_map/all_to_all | solution.py:138
  109.5 10.8 %all-to-all-start.2 = ((bf16[2,128,768]{1,0,2:T(2,128)(2,1)}), bf16[2,128,768]{1,0,2:T(2,128)(2,1)S(1)}, u32[]{:S(2)}, u32[]{:S(2)}) async-start(bf16[2,128,768]{1,0,2:T(2,128)(2,1)} %copy.117), calls=%async_computation.2 | async-start | bytes 786432 | tf_op jit(solution)/shard_map/all_to_all | solution.py:137
  129.5 42.2 %all-to-all-start.3 = ((bf16[2,512,192]{2,0,1:T(2,128)(2,1)}), bf16[2,512,192]{2,0,1:T(2,128)(2,1)S(1)}, u32[]{:S(2)}, u32[]{:S(2)}) async-start(bf16[2,512,192]{2,0,1:T(2,128)(2,1)} %copy.120), calls=%async_computation.3 | async-start | bytes 1048576 | tf_op jit(solution)/shard_map/all_to_all | solution.py:158
  318.0 10.8 %all-to-all-start.4 = ((bf16[2,128,768]{1,0,2:T(2,128)(2,1)}), bf16[2,128,768]{1,0,2:T(2,128)(2,1)S(1)}, u32[]{:S(2)}, u32[]{:S(2)}) async-start(bf16[2,128,768]{1,0,2:T(2,128)(2,1)} %copy.123), calls=%async_computation.4 | async-start | bytes 786432 | tf_op jit(solution)/shard_map/all_to_all | solution.py:187
  321.4 138.8 %reduce-scatter.13.cloned.1.call-start = ((), (), s32[]{:S(2)}) async-start(), calls=%async_computation.19 | async-start | bytes 2654208 | tf_op jit(solution)/shard_map/reduce_scatter | solution.py:263
  323.4 143.4 %reduce-scatter.19.cloned.1.call-start = ((), (), s32[]{:S(2)}) async-start(), calls=%async_computation.22 | async-start | bytes 2654208
  361.5 177.7 %reduce-scatter.21.cloned.1.call-start = ((), (), s32[]{:S(2)}) async-start(), calls=%async_computation.23 | async-start | bytes 2654208
  378.7 232.8 %reduce-scatter.23.cloned.1.call-start = ((), (), s32[]{:S(2)}) async-start(), calls=%async_computation.24 | async-start | bytes 2654208
  396.3 380.0 %reduce-scatter.15.cloned.1.call-start = ((), (), s32[]{:S(2)}) async-start(), calls=%async_computation.20 | async-start | bytes 10616832 | tf_op jit(solution)/shard_map/reduce_scatter | solution.py:267
  404.0 537.1 %reduce-scatter.17.cloned.1.call-start = ((), (), s32[]{:S(2)}) async-start(), calls=%async_computation.21 | async-start | bytes 10616832 | tf_op jit(solution)/shard_map/reduce_scatter | solution.py:269
  410.6 582.1 %all-reduce.23.cloned.1.call-start = ((), (), s32[]{:S(2)}) async-start(), calls=%async_computation.25 | async-start | bytes 3833856 | tf_op jit(solution)/shard_map/psum | solution.py:275
  (47 other events, 1556.6 us)
Sparse Core Ops, SparseCore 0:
  10.2 43.8 all-gather.6
  56.3 44.0 all-gather.8
  102.6 39.7 all-gather.10
  144.5 78.1 all-gather.12
  224.7 77.6 all-gather.14
  325.4 68.4 reduce-scatter.12
  397.4 69.3 reduce-scatter.18
  470.2 68.8 reduce-scatter.20
  542.6 68.8 reduce-scatter.22
  614.9 161.3 reduce-scatter.14
  779.9 161.1 reduce-scatter.16
  944.9 47.7 all-reduce.22
